TPU v7x, 256 devices: a whole 4x4x8 slice. The times are simulated.
256 devices in a mesh: tok: 16 (over y, x), ch: 16 (over z, core).
Axes of the slice: x: 4, y: 4, z: 8, core: 2. Of those that a mesh axis runs over, the one named last changes fastest.
Arguments:
- tokens: bfloat16 [256, 16384], P('tok', 'ch'), may hold values from -64 to 64
- probe: int32 [256, 16384], P('tok', 'ch'), may hold values from 0 to 1
- signs: int32 [16384], P('ch'), may hold values from 0 to 1
- gate_weight: bfloat16 [16384, 26624], P('ch', 'tok'), may hold values from -0.046875 to 0.046875
- up_weight: bfloat16 [16384, 26624], P('ch', 'tok'), may hold values from -0.046875 to 0.046875
- down_weight: bfloat16 [26624, 16384], P('tok', 'ch'), may hold values from -0.0390625 to 0.0390625
Outputs:
- rotated_product: float32 [256, 16384], P('tok', 'ch')
- diagonal_estimate: float32 [16384], P('ch')
All inputs are finite; a program needn't handle non-finite values.
Results may differ from a plain program's by a relative error of at most 0.004.
Values may be sent and summed in bfloat16 or wider, within the bound.
No kernel may reach another device: no remote copies, remote signals or barrier semaphores. Data moves between devices by JAX's collectives and lax.ppermute only.
A program may use at most 128 MiB of HBM per device.

v0:
```python
import math
import jax
import jax.numpy as jnp
from jax import lax
from jax.sharding import PartitionSpec as P

D = 16384


def partner_2(value, axis, stride):
    mask = 2**stride
    pairs = [(source, source ^ mask) for source in range(lax.axis_size(axis))]
    return lax.ppermute(value, axis, pairs)


def sign_table(length):
    indices = jnp.arange(length, dtype=jnp.int32)
    parity = jnp.zeros((length, length), jnp.int32)
    for bit_pos in range(length.bit_length() - 1):
        parity = parity + (indices[:, None] >> bit_pos & 1) * (indices[None, :] >> bit_pos & 1)
    return jnp.where(parity % 2 == 0, 1.0, -1.0).astype(jnp.float32)


def cross_pairs(values):
    my_index = lax.axis_index("ch")
    for bit_pos in range(lax.axis_size("ch").bit_length() - 1):
        partner = partner_2(values, "ch", bit_pos)
        upper_half = my_index >> bit_pos & 1 == 1
        values = jnp.where(upper_half, partner - values, values + partner)
    return values


def cross_section(values):
    return cross_pairs(values)


def grad_product(gate_piece, up_piece, gate_weight, up_weight):
    contract = (((1,), (1,)), ((), ()))
    first_term = lax.dot_general(
        gate_piece, gate_weight, contract, preferred_element_type=jnp.float32
    )
    return first_term + lax.dot_general(
        up_piece, up_weight, contract, preferred_element_type=jnp.float32
    )


def on_device(tokens, probe, signs, gate_weight, up_weight, down_weight):
    tok_rows, channels = tokens.shape
    total_rows = tok_rows * lax.axis_size("tok")
    root_scale = 1.0 / math.sqrt(D)
    hadamard = sign_table(channels)
    probe_signs = (2 * probe - 1).astype(jnp.float32)
    channel_signs = (2 * signs - 1).astype(jnp.float32)
    start_local = jnp.dot(
        (probe_signs * channel_signs[None, :]).astype(jnp.bfloat16),
        hadamard.astype(jnp.bfloat16),
        preferred_element_type=jnp.float32,
    )
    tangent = (cross_section(start_local) * root_scale).astype(jnp.bfloat16)
    all_tokens, all_tangent = (
        lax.all_gather(tokens, "tok", axis=0, tiled=True),
        lax.all_gather(tangent, "tok", axis=0, tiled=True),
    )
    inputs = jnp.stack([all_tokens, all_tangent], axis=1)
    gate_part = jnp.einsum("rsd,df->rsf", inputs, gate_weight, preferred_element_type=jnp.float32)
    up_part = jnp.einsum("rsd,df->rsf", inputs, up_weight, preferred_element_type=jnp.float32)
    summed = lax.psum_scatter(
        jnp.stack([gate_part, up_part], axis=2), "ch", scatter_dimension=0, tiled=True
    )
    gate_pre = summed[:, 0, 0]
    up_pre = summed[:, 0, 1]
    gate_tan = summed[:, 1, 0]
    up_tan = summed[:, 1, 1]
    sigmoid_gate = jax.nn.sigmoid(gate_pre)
    activated = gate_pre * sigmoid_gate
    slope_term = sigmoid_gate * (1.0 + gate_pre * (1.0 - sigmoid_gate))
    hidden_tan = (slope_term * gate_tan * up_pre + activated * up_tan).astype(jnp.bfloat16)
    out_part = jnp.dot(
        lax.all_gather(hidden_tan, "ch", axis=0, tiled=True),
        down_weight,
        preferred_element_type=jnp.float32,
    )
    out_tangent = lax.psum(out_part, "tok").astype(jnp.bfloat16)
    piece = out_tangent
    back_hidden = lax.psum_scatter(
        lax.dot_general(
            piece, down_weight, (((1,), (1,)), ((), ())), preferred_element_type=jnp.float32
        ),
        "ch",
        scatter_dimension=0,
        tiled=True,
    )
    back_gate = (back_hidden * up_pre * slope_term).astype(jnp.bfloat16)
    back_up = (back_hidden * activated).astype(jnp.bfloat16)
    stacked = jnp.stack([back_gate, back_up], axis=1)
    piece = lax.all_gather(stacked, "ch", axis=0, tiled=True)
    in_part = grad_product(piece[:, 0], piece[:, 1], gate_weight, up_weight)
    back_tokens = lax.psum_scatter(in_part, "tok", scatter_dimension=0, tiled=True)
    local_back = jnp.dot(
        back_tokens, hadamard, precision=lax.Precision.HIGHEST, preferred_element_type=jnp.float32
    )
    rotated_product = cross_section(local_back) * root_scale * channel_signs[None, :]
    token_terms = jnp.sum(probe_signs * rotated_product, axis=0)
    diagonal_estimate = lax.psum(token_terms, "tok") / total_rows
    return (rotated_product, diagonal_estimate)


def solution(mesh):
    placed = (
        P("tok", "ch"),
        P("tok", "ch"),
        P("ch"),
        P("ch", "tok"),
        P("ch", "tok"),
        P("tok", "ch"),
    )
    return jax.shard_map(
        on_device, mesh=mesh, in_specs=placed, out_specs=(P("tok", "ch"), P("ch")), check_vma=False
    )
```

profile of v0, /device:TPU:32, one launch (start us, length us, event | category | flops | bytes accessed | tf_op | source)
XLA Modules:
  0.0 515.5 jit_solution(10228923519675699118)
XLA Ops:
  7.2 0.0 copy-start
  7.2 0.0 reduce-scatter.4.cloned.1.call-start
  7.3 0.8 add_convert_fusion
  8.1 6.5 %fusion.3 = pred[1024,1024]{1,0:T(32,128)(4,1)S(1)} fusion(s32[1024]{0:T(1024)S(1)} %get-tuple-element.6, s32[1024]{0:T(1024)S(1)} %get-tuple-element.7, s32[1024]{0:T(1024)S(1)} %get-tuple-element.8, s32[1024]{0:T(1024)S(1)} %get-tuple-element.9, s32[1024]{0:T(1024)S(1)} %get-tuple-element.10, s32[1024]{0:T(1024)S(1)} %get-tuple-element.11, ...), kind=kLoop, calls=%fused_computation.8 | loop fusion | flops 32505856 | bytes 1089536 | tf_op jit(solution)/shard_map/eq | solution.py:21
  14.6 0.0 copy-start.1
  14.6 1.0 copy-done.1
  15.6 1.4 fusion.14
  17.0 0.0 collective-permute-start
  17.0 1.4 collective-permute-done
  18.4 0.8 add_select_fusion.6
  19.2 1.9 collective-permute-start.1
  21.2 2.5 collective-permute-done.1
  23.7 0.8 add_select_fusion.5
  24.5 3.4 collective-permute-start.2
  27.9 2.3 collective-permute-done.2
  30.2 6.1 %collective-permute-start.3 = (f32[16,1024]{1,0:T(8,128)S(1)}, f32[16,1024]{1,0:T(8,128)S(1)}, u32[]{:S(2)}, u32[]{:S(2)}) collective-permute-start(f32[16,1024]{1,0:T(8,128)S(1)} %add_select_fusion.4), channel_id=1, source_target_pairs={{0,8},{1,9},{2,10},{3,11},{4,12},{5,13},{6,14},{7,15},{8,0},{9,1},... | collective-permute-start | bytes 196616 | tf_op jit(solution)/shard_map/ppermute | solution.py:13
  36.3 24.4 %all_gather.12 = bf16[256,1024]{1,0:T(8,128)(2,1)S(1)} all-gather(bf16[16,1024]{1,0:T(8,128)(2,1)} %param.6), channel_id=1, replica_groups=mesh['tok'=16,'ch'=16] {'tok'}, dimensions={0}, use_global_device_ids=true | all-gather | bytes 557056 | tf_op jit(solution)/shard_map/all_gather | solution.py:61
  60.6 0.0 collective-permute-done.3
  60.7 23.3 %all_gather.13 = bf16[256,1024]{1,0:T(8,128)(2,1)S(1)} all-gather(bf16[16,1024]{1,0:T(8,128)(2,1)S(1)} %multiply_convert_fusion.2), channel_id=1, replica_groups=mesh['tok'=16,'ch'=16] {'tok'}, dimensions={0}, use_global_device_ids=true | all-gather | bytes 557056 | tf_op jit(solution)/shard_map/all_gather | solution.py:62
  84.0 4.0 fusion.11
  88.0 0.0 copy-done
  88.0 2.1 fusion.8
  90.1 3.3 pad_maximum_fusion
  93.4 0.0 reduce-scatter.4.cloned.1.call-update
  93.4 0.0 reduce-scatter.6.cloned.1.call-start
  93.4 60.3 %reduce-scatter.4.cloned.1.call-done = f32[16,2,2,1664]{3,0,1,2:T(8,128)} async-done(((f32[256,2,2,1664]{3,0,1,2:T(8,128)}), f32[16,2,2,1664]{3,0,1,2:T(8,128)}) %reduce-scatter.4.cloned.1.call-update) | async-done | bytes 426000 | tf_op jit(solution)/shard_map/reduce_scatter | solution.py:67
  153.7 1.1 fusion.24
  154.8 20.4 %all_gather.14 = bf16[256,1664]{1,0:T(8,128)(2,1)S(1)} all-gather(bf16[16,1664]{1,0:T(8,128)(2,1)S(1)} %fusion.24), channel_id=1, replica_groups=mesh['tok'=16,'ch'=16] {'ch'}, dimensions={0}, use_global_device_ids=true | all-gather | bytes 905216 | tf_op jit(solution)/shard_map/all_gather | solution.py:79
  175.3 4.1 fusion.41
  179.4 88.3 %all-reduce.1 = bf16[256,1024]{1,0:T(8,128)(2,1)} all-reduce(f32[256,1024]{1,0:T(8,128)} %fusion.41), channel_id=1, replica_groups=mesh['tok'=16,'ch'=16] {'tok'}, use_global_device_ids=true, to_apply=%region_1.2 | all-reduce | flops 262144 | bytes 1572864 | tf_op jit(solution)/shard_map/psum | solution.py:83
  267.7 4.5 fusion.42
  272.2 0.0 reduce-scatter.6.cloned.1.call-update
  272.2 0.0 all-gather.2.cloned.1.call-start
  272.3 49.8 %reduce-scatter.6.cloned.1.call-done = f32[16,1664]{1,0:T(8,128)} async-done(((f32[256,1664]{1,0:T(8,128)}), f32[16,1664]{1,0:T(8,128)}) %reduce-scatter.6.cloned.1.call-update) | async-done | bytes 106512 | tf_op jit(solution)/shard_map/reduce_scatter | solution.py:85
  322.1 1.1 fusion.28
  323.1 0.7 pad_maximum_fusion.4
  323.8 0.0 all-gather.2.cloned.1.call-update
  323.8 0.2 reduce-scatter.8.cloned.1.call-start
  324.1 40.5 %all-gather.2.cloned.1.call-done = bf16[256,2,1664]{2,0,1:T(8,128)(2,1)} async-done(((bf16[16,2,1664]{2,0,1:T(8,128)(2,1)}), bf16[256,2,1664]{2,0,1:T(8,128)(2,1)}) %all-gather.2.cloned.1.call-update) | async-done | bytes 1703952 | tf_op jit(solution)/shard_map/all_gather | solution.py:96
  364.6 0.0 copy-start.4
  364.6 0.0 copy-start.5
  364.6 2.4 fusion.19
  367.0 0.0 copy-done.4
  367.0 0.3 copy-done.5
  367.3 0.0 copy-start.3
  367.3 0.0 copy-start.2
  367.3 2.1 convolution_add_fusion
  369.5 0.0 reduce-scatter.8.cloned.1.call-update
  369.5 77.1 %reduce-scatter.8.cloned.1.call-done = f32[16,1024]{1,0:T(8,128)} async-done(((f32[256,1024]{1,0:T(8,128)}), f32[16,1024]{1,0:T(8,128)}) %reduce-scatter.8.cloned.1.call-update) | async-done | bytes 65552 | tf_op jit(solution)/shard_map/reduce_scatter | solution.py:98
  446.6 3.6 fusion
  450.2 0.0 collective-permute-start.4
  450.2 1.2 collective-permute-done.4
  451.4 0.5 collective-permute-start.5
  452.0 3.8 collective-permute-done.5
  455.8 2.6 collective-permute-start.6
  458.4 2.6 collective-permute-done.6
  461.1 5.0 collective-permute-start.7
  466.1 0.0 copy-done.3
  466.1 3.5 collective-permute-done.7
  469.6 0.0 copy-done.2
  469.6 0.7 multiply_reduce_fusion
  470.3 38.1 %psum.15 = f32[1024]{0:T(1024)S(1)} all-reduce(f32[1024]{0:T(1024)S(1)} %get-tuple-element.2), channel_id=1, replica_groups=mesh['tok'=16,'ch'=16] {'tok'}, use_global_device_ids=true, to_apply=%region_5.6 | all-reduce | flops 1024 | bytes 8192 | tf_op jit(solution)/shard_map/psum | solution.py:104
  508.4 0.6 broadcast_multiply_fusion
  (11 shorter events, 0.1 us)
Async XLA Ops:
  7.2 80.8 %copy-start = (bf16[1024,1664]{1,0:T(8,128)(2,1)S(1)}, bf16[1024,1664]{1,0:T(8,128)(2,1)}, u32[]{:S(2)}) copy-start(bf16[1024,1664]{1,0:T(8,128)(2,1)} %param.9) | copy-start | bytes 10223620
  7.2 146.5 %reduce-scatter.4.cloned.1.call-start = ((), (), s32[]{:S(2)}) async-start(), calls=%async_computation.3 | async-start | bytes 7241728 | tf_op jit(solution)/shard_map/reduce_scatter | solution.py:67
  14.6 1.0 copy-start.1
  17.0 1.4 collective-permute-start
  19.2 4.5 collective-permute-start.1
  24.5 5.7 %collective-permute-start.2 = (f32[16,1024]{1,0:T(8,128)S(1)}, f32[16,1024]{1,0:T(8,128)S(1)}, u32[]{:S(2)}, u32[]{:S(2)}) collective-permute-start(f32[16,1024]{1,0:T(8,128)S(1)} %add_select_fusion.5), channel_id=1, source_target_pairs={{0,4},{1,5},{2,6},{3,7},{4,0},{5,1},{6,2},{7,3},{8,12},{9,13},{10,... | collective-permute-start | bytes 196616 | tf_op jit(solution)/shard_map/ppermute | solution.py:13
  30.2 30.4 %collective-permute-start.3 = (f32[16,1024]{1,0:T(8,128)S(1)}, f32[16,1024]{1,0:T(8,128)S(1)}, u32[]{:S(2)}, u32[]{:S(2)}) collective-permute-start(f32[16,1024]{1,0:T(8,128)S(1)} %add_select_fusion.4), channel_id=1, source_target_pairs={{0,8},{1,9},{2,10},{3,11},{4,12},{5,13},{6,14},{7,15},{8,0},{9,1},... | collective-permute-start | bytes 196616 | tf_op jit(solution)/shard_map/ppermute | solution.py:13
  93.4 228.7 %reduce-scatter.6.cloned.1.call-start = ((), (), s32[]{:S(2)}) async-start(), calls=%async_computation.4 | async-start | bytes 1810432 | tf_op jit(solution)/shard_map/reduce_scatter | solution.py:85
  272.2 92.4 %all-gather.2.cloned.1.call-start = ((), (), s32[]{:S(2)}) async-start(), calls=%async_computation.5 | async-start | bytes 1810432 | tf_op jit(solution)/shard_map/all_gather | solution.py:96
  323.8 122.8 %reduce-scatter.8.cloned.1.call-start = ((), (), s32[]{:S(2)}) async-start(), calls=%async_computation.6 | async-start | bytes 1114112 | tf_op jit(solution)/shard_map/reduce_scatter | solution.py:98
  364.6 2.5 copy-start.4
  364.6 2.7 copy-start.5
  367.3 98.8 %copy-start.3 = (s32[1024]{0:T(1024)S(1)}, s32[1024]{0:T(1024)}, u32[]{:S(2)}) copy-start(s32[1024]{0:T(1024)} %param.8) | copy-start | bytes 12292
  367.3 102.3 %copy-start.2 = (s32[16,1024]{1,0:T(8,128)S(1)}, s32[16,1024]{1,0:T(8,128)}, u32[]{:S(2)}) copy-start(s32[16,1024]{1,0:T(8,128)} %param.7) | copy-start | bytes 196612
  450.2 1.3 collective-permute-start.4
  451.4 4.4 collective-permute-start.5
  455.8 5.3 %collective-permute-start.6 = (f32[16,1024]{1,0:T(8,128)S(1)}, f32[16,1024]{1,0:T(8,128)S(1)}, u32[]{:S(2)}, u32[]{:S(2)}) collective-permute-start(f32[16,1024]{1,0:T(8,128)S(1)} %add_select_fusion.2), channel_id=1, source_target_pairs={{0,4},{1,5},{2,6},{3,7},{4,0},{5,1},{6,2},{7,3},{8,12},{9,13},{10,... | collective-permute-start | bytes 196616 | tf_op jit(solution)/shard_map/ppermute | solution.py:13
  461.1 8.5 %collective-permute-start.7 = (f32[16,1024]{1,0:T(8,128)S(1)}, f32[16,1024]{1,0:T(8,128)S(1)}, u32[]{:S(2)}, u32[]{:S(2)}) collective-permute-start(f32[16,1024]{1,0:T(8,128)S(1)} %add_select_fusion.1), channel_id=1, source_target_pairs={{0,8},{1,9},{2,10},{3,11},{4,12},{5,13},{6,14},{7,15},{8,0},{9,1},... | collective-permute-start | bytes 196616 | tf_op jit(solution)/shard_map/ppermute | solution.py:13
Sparse Core Ops, SparseCore 0:
  93.5 60.1 reduce-scatter.3
  272.3 49.7 reduce-scatter.5
  324.1 40.4 all-gather.1
  369.6 76.9 reduce-scatter.7
where the time goes:
time: 516 us
  waiting for transfers between devices  245 us (47%)
  blocking collectives  195 us (38%)
  matrix products  24.3 us (5%)
  starting transfers between devices  19.8 us (4%)
  other arithmetic  16.4 us (3%)
  between operations  13.9 us (3%)
    psum x1, blocking collectives, on_device(): out_tangent = lax.psum(out_part, 'tok').astype(jnp.bfloat16)  88.3 us
    reduce_scatter x1, waiting for transfers between devices, on_device(): lax.psum_scatter(in_part, 'tok', scatter_dimension=0, tiled=True)  77.1 us
    reduce_scatter x1, waiting for transfers between devices, on_device(): lax.psum_scatter(jnp.stack([gate_part, up_part], axis=2), 'ch', scatter_d...  60.3 us
    reduce_scatter x1, waiting for transfers between devices, on_device(): lax.psum_scatter(lax.dot_general(piece, down_weight, (((1,), (1,)), ((),...  49.8 us
    all_gather x1, waiting for transfers between devices, on_device(): piece = lax.all_gather(stacked, 'ch', axis=0, tiled=True)  40.5 us
    psum x1, blocking collectives, on_device(): diagonal_estimate = lax.psum(token_terms, 'tok') / total_rows  38.1 us
    all_gather x1, blocking collectives, on_device(): lax.all_gather(tokens, 'tok', axis=0, tiled=True)  24.4 us
    all_gather x1, blocking collectives, on_device(): lax.all_gather(tangent, 'tok', axis=0, tiled=True)  23.3 us
  transfers between devices with their start and end apart: 12, of which 11 were waited for; matrix products, arithmetic and copies ran while one was open for 0% of the time, Pallas kernels for 0%

commit v1 on v0

--- a/solution.py
+++ b/solution.py
@@ -5,6 +5,28 @@
 from jax.sharding import PartitionSpec as P
 
 D = 16384
+
+
+def laid_out(blocks, dim):
+    shape = list(blocks.shape[1:])
+    shape[dim] *= blocks.shape[0]
+    return jnp.moveaxis(blocks, 0, dim).reshape(shape)
+
+
+def ring_gather(array, axis, dim):
+    count = lax.axis_size(axis)
+    pairs = [(i, (i + 1) % count) for i in range(count)]
+    back = [(b, a) for a, b in pairs]
+    lower, upper = ([], [])
+    for turn in range(count - 1):
+        if turn % 2 == 0:
+            lower.append(lax.ppermute(lower[-1] if lower else array, axis, pairs))
+        else:
+            upper.append(lax.ppermute(upper[-1] if upper else array, axis, back))
+    parts = jnp.stack([*lower[::-1], array, *upper])
+    shift = lax.axis_index(axis) - len(lower)
+    parts = parts[(jnp.arange(count) - shift) % count]
+    return laid_out(parts, dim)
 
 
 def partner_2(value, axis, stride):
@@ -93,7 +115,7 @@
     back_gate = (back_hidden * up_pre * slope_term).astype(jnp.bfloat16)
     back_up = (back_hidden * activated).astype(jnp.bfloat16)
     stacked = jnp.stack([back_gate, back_up], axis=1)
-    piece = lax.all_gather(stacked, "ch", axis=0, tiled=True)
+    piece = ring_gather(stacked, "ch", 0)
     in_part = grad_product(piece[:, 0], piece[:, 1], gate_weight, up_weight)
     back_tokens = lax.psum_scatter(in_part, "tok", scatter_dimension=0, tiled=True)
     local_back = jnp.dot(

time: 516 us -> 545 us (1.056)
  local copies, waits for them, and re-layouts: 1.26 us -> 26.7 us
  starting transfers between devices: 19.8 us -> 38.6 us
  waiting for transfers between devices: 245 us -> 231 us
    all_gather x1 -> x0, waiting for transfers between devices: 40.5 us -> none  [on_device(): piece = lax.all_gather(stacked, 'ch', axis=0, tiled=True)]
    ppermute x0 -> x15, waiting for transfers between devices: none -> 20.1 us  [the longest x8 16.6 us: ring_gather(): lower.append(lax.ppermute(lower[-1] if lower else array, axis, pairs))]
    unnamed x12 -> x36, local copies, waits for them, and re-layouts: 1.26 us -> 21.1 us
    ppermute x0 -> x15, starting transfers between devices: none -> 18.8 us  [the longest x7 18.7 us: ring_gather(): upper.append(lax.ppermute(upper[-1] if upper else array, axis, back))]
    reduce_scatter x1, waiting for transfers between devices: 77.1 us -> 83.3 us  [on_device(): lax.psum_scatter(in_part, 'tok', scatter_dimension=0, tiled=True)]
  transfers between devices with their start and end apart: 12 -> 26, of which waited for: 11 -> 23; matrix products, arithmetic and copies ran while one was open for 0% -> 3% of each run, Pallas kernels for 0% -> 0%
where the time goes in v1:
time: 545 us; the launch traced here: 544 us
  waiting for transfers between devices  231 us (42%)
  blocking collectives  194 us (36%)
  starting transfers between devices  38.6 us (7%)
  local copies, waits for them, and re-layouts  26.7 us (5%)
  matrix products  23 us (4%)
  other arithmetic  16.4 us (3%)
  between operations  13.9 us (3%)
    psum x1, blocking collectives, on_device(): out_tangent = lax.psum(out_part, 'tok').astype(jnp.bfloat16)  88.2 us
    reduce_scatter x1, waiting for transfers between devices, on_device(): lax.psum_scatter(in_part, 'tok', scatter_dimension=0, tiled=True)  83.3 us
    reduce_scatter x1, waiting for transfers between devices, on_device(): lax.psum_scatter(jnp.stack([gate_part, up_part], axis=2), 'ch', scatter_d...  60.2 us
    reduce_scatter x1, waiting for transfers between devices, on_device(): lax.psum_scatter(lax.dot_general(piece, down_weight, (((1,), (1,)), ((),...  49.8 us
    psum x1, blocking collectives, on_device(): diagonal_estimate = lax.psum(token_terms, 'tok') / total_rows  38.1 us
    all_gather x1, blocking collectives, on_device(): lax.all_gather(tokens, 'tok', axis=0, tiled=True)  24.4 us
    all_gather x1, blocking collectives, on_device(): lax.all_gather(tangent, 'tok', axis=0, tiled=True)  23.3 us
    unnamed x36, local copies, waits for them, and re-layouts  21.1 us
  transfers between devices with their start and end apart: 26, of which 23 were waited for; matrix products, arithmetic and copies ran while one was open for 3% of the time, Pallas kernels for 0%

profile of v1, /device:TPU:32, one launch (start us, length us, event | category | flops | bytes accessed | tf_op | source)
XLA Modules:
  0.0 544.1 jit_solution(18397620331970088893)
XLA Ops:
  7.3 0.8 add_convert_fusion
  8.1 6.5 %fusion.3 = pred[1024,1024]{1,0:T(32,128)(4,1)S(1)} fusion(s32[1024]{0:T(1024)S(1)} %get-tuple-element.6, s32[1024]{0:T(1024)S(1)} %get-tuple-element.7, s32[1024]{0:T(1024)S(1)} %get-tuple-element.8, s32[1024]{0:T(1024)S(1)} %get-tuple-element.9, s32[1024]{0:T(1024)S(1)} %get-tuple-element.10, s32[1024]{0:T(1024)S(1)} %get-tuple-element.11, ...), kind=kLoop, calls=%fused_computation.9 | loop fusion | flops 32505856 | bytes 1089536 | tf_op jit(solution)/shard_map/eq | solution.py:43
  14.6 1.0 copy-done.1
  15.6 1.4 fusion.14
  17.0 1.4 collective-permute-done
  18.4 0.8 add_select_fusion.6
  19.3 1.9 collective-permute-start.1
  21.2 2.5 collective-permute-done.1
  23.7 0.8 add_select_fusion.5
  24.6 3.4 collective-permute-start.2
  27.9 2.3 collective-permute-done.2
  30.3 6.1 %collective-permute-start.3 = (f32[16,1024]{1,0:T(8,128)S(1)}, f32[16,1024]{1,0:T(8,128)S(1)}, u32[]{:S(2)}, u32[]{:S(2)}) collective-permute-start(f32[16,1024]{1,0:T(8,128)S(1)} %add_select_fusion.4), channel_id=1, source_target_pairs={{0,8},{1,9},{2,10},{3,11},{4,12},{5,13},{6,14},{7,15},{8,0},{9,1},... | collective-permute-start | bytes 196616 | tf_op jit(solution)/shard_map/ppermute | solution.py:35
  36.3 24.4 %all_gather.9 = bf16[256,1024]{1,0:T(8,128)(2,1)S(1)} all-gather(bf16[16,1024]{1,0:T(8,128)(2,1)} %param.6), channel_id=1, replica_groups=mesh['tok'=16,'ch'=16] {'tok'}, dimensions={0}, use_global_device_ids=true | all-gather | bytes 557056 | tf_op jit(solution)/shard_map/all_gather | solution.py:83
  60.7 23.3 %all_gather.10 = bf16[256,1024]{1,0:T(8,128)(2,1)S(1)} all-gather(bf16[16,1024]{1,0:T(8,128)(2,1)S(1)} %multiply_convert_fusion.2), channel_id=1, replica_groups=mesh['tok'=16,'ch'=16] {'tok'}, dimensions={0}, use_global_device_ids=true | all-gather | bytes 557056 | tf_op jit(solution)/shard_map/all_gather | solution.py:84
  84.0 4.0 fusion.11
  88.0 2.1 fusion.8
  90.1 3.2 pad_maximum_fusion
  93.4 60.2 %reduce-scatter.4.cloned.1.call-done = f32[16,2,2,1664]{3,0,1,2:T(8,128)} async-done(((f32[256,2,2,1664]{3,0,1,2:T(8,128)}), f32[16,2,2,1664]{3,0,1,2:T(8,128)}) %reduce-scatter.4.cloned.1.call-update) | async-done | bytes 426000 | tf_op jit(solution)/shard_map/reduce_scatter | solution.py:89
  153.6 1.1 fusion.24
  154.8 20.4 %all_gather.11 = bf16[256,1664]{1,0:T(8,128)(2,1)S(1)} all-gather(bf16[16,1664]{1,0:T(8,128)(2,1)S(1)} %fusion.24), channel_id=1, replica_groups=mesh['tok'=16,'ch'=16] {'ch'}, dimensions={0}, use_global_device_ids=true | all-gather | bytes 905216 | tf_op jit(solution)/shard_map/all_gather | solution.py:101
  175.2 4.1 fusion.43
  179.3 88.2 %all-reduce.1 = bf16[256,1024]{1,0:T(8,128)(2,1)} all-reduce(f32[256,1024]{1,0:T(8,128)} %fusion.43), channel_id=1, replica_groups=mesh['tok'=16,'ch'=16] {'tok'}, use_global_device_ids=true, to_apply=%region_1.2 | all-reduce | flops 262144 | bytes 1572864 | tf_op jit(solution)/shard_map/psum | solution.py:105
  267.5 4.5 fusion.44
  272.3 49.8 %reduce-scatter.6.cloned.1.call-done = f32[16,1664]{1,0:T(8,128)} async-done(((f32[256,1664]{1,0:T(8,128)}), f32[16,1664]{1,0:T(8,128)}) %reduce-scatter.6.cloned.1.call-update) | async-done | bytes 106512 | tf_op jit(solution)/shard_map/reduce_scatter | solution.py:107
  322.1 1.1 fusion.28
  323.2 4.1 collective-permute-done.4
  328.0 1.7 collective-permute-start.12
  329.7 2.4 collective-permute-done.5
  332.8 1.7 collective-permute-start.13
  334.5 1.7 collective-permute-done.6
  336.8 3.1 collective-permute-start.14
  339.9 1.6 collective-permute-done.7
  342.2 3.1 collective-permute-start.15
  345.3 1.7 collective-permute-done.8
  346.9 0.9 collective-permute-done.15
  347.9 2.9 collective-permute-start.16
  350.8 1.8 collective-permute-done.9
  353.4 3.0 collective-permute-start.17
  356.4 1.7 collective-permute-done.10
  358.7 3.2 collective-permute-start.18
  361.9 1.6 collective-permute-done.11
  364.8 1.5 bitcast_dynamic-update-slice_fusion.13
  366.3 1.5 bitcast_dynamic-update-slice_fusion.12
  367.8 1.6 bitcast_dynamic-update-slice_fusion.11
  369.4 1.5 bitcast_dynamic-update-slice_fusion.10
  370.9 1.5 bitcast_dynamic-update-slice_fusion.9
  372.5 1.5 bitcast_dynamic-update-slice_fusion.8
  374.7 1.5 bitcast_dynamic-update-slice_fusion.6
  376.2 1.5 bitcast_dynamic-update-slice_fusion.5
  377.8 1.5 bitcast_dynamic-update-slice_fusion.4
  379.3 1.5 bitcast_dynamic-update-slice_fusion.3
  382.8 3.4 gather_fusion
  386.2 1.6 copy.14
  387.8 1.2 fusion.19
  389.7 2.1 convolution_add_fusion
  391.9 83.3 %reduce-scatter.8.cloned.1.call-done = f32[16,1024]{1,0:T(8,128)} async-done(((f32[256,1024]{1,0:T(8,128)}), f32[16,1024]{1,0:T(8,128)}) %reduce-scatter.8.cloned.1.call-update) | async-done | bytes 65552 | tf_op jit(solution)/shard_map/reduce_scatter | solution.py:120
  475.2 3.6 fusion
  478.8 1.2 collective-permute-done.19
  480.6 3.8 collective-permute-done.20
  484.4 2.6 collective-permute-start.21
  487.0 2.6 collective-permute-done.21
  489.7 5.0 collective-permute-start.22
  494.7 3.5 collective-permute-done.22
  498.9 38.1 %psum.15 = f32[1024]{0:T(1024)S(1)} all-reduce(f32[1024]{0:T(1024)S(1)} %get-tuple-element.2), channel_id=1, replica_groups=mesh['tok'=16,'ch'=16] {'tok'}, use_global_device_ids=true, to_apply=%region_5.6 | all-reduce | flops 1024 | bytes 8192 | tf_op jit(solution)/shard_map/psum | solution.py:126
  (67 shorter events, 11.0 us)
Async XLA Ops:
  7.2 80.9 %copy-start = (bf16[1024,1664]{1,0:T(8,128)(2,1)S(1)}, bf16[1024,1664]{1,0:T(8,128)(2,1)}, u32[]{:S(2)}) copy-start(bf16[1024,1664]{1,0:T(8,128)(2,1)} %param.9) | copy-start | bytes 10223620
  7.2 146.5 %reduce-scatter.4.cloned.1.call-start = ((), (), s32[]{:S(2)}) async-start(), calls=%async_computation.3 | async-start | bytes 7241728 | tf_op jit(solution)/shard_map/reduce_scatter | solution.py:89
  14.6 1.0 copy-start.1
  17.0 1.4 collective-permute-start
  19.3 4.5 collective-permute-start.1
  24.6 5.7 %collective-permute-start.2 = (f32[16,1024]{1,0:T(8,128)S(1)}, f32[16,1024]{1,0:T(8,128)S(1)}, u32[]{:S(2)}, u32[]{:S(2)}) collective-permute-start(f32[16,1024]{1,0:T(8,128)S(1)} %add_select_fusion.5), channel_id=1, source_target_pairs={{0,4},{1,5},{2,6},{3,7},{4,0},{5,1},{6,2},{7,3},{8,12},{9,13},{10,... | collective-permute-start | bytes 196616 | tf_op jit(solution)/shard_map/ppermute | solution.py:35
  30.3 30.4 %collective-permute-start.3 = (f32[16,1024]{1,0:T(8,128)S(1)}, f32[16,1024]{1,0:T(8,128)S(1)}, u32[]{:S(2)}, u32[]{:S(2)}) collective-permute-start(f32[16,1024]{1,0:T(8,128)S(1)} %add_select_fusion.4), channel_id=1, source_target_pairs={{0,8},{1,9},{2,10},{3,11},{4,12},{5,13},{6,14},{7,15},{8,0},{9,1},... | collective-permute-start | bytes 196616 | tf_op jit(solution)/shard_map/ppermute | solution.py:35
  93.4 228.7 %reduce-scatter.6.cloned.1.call-start = ((), (), s32[]{:S(2)}) async-start(), calls=%async_computation.4 | async-start | bytes 1810432 | tf_op jit(solution)/shard_map/reduce_scatter | solution.py:107
  272.1 203.1 %reduce-scatter.8.cloned.1.call-start = ((), (), s32[]{:S(2)}) async-start(), calls=%async_computation.5 | async-start | bytes 1114112 | tf_op jit(solution)/shard_map/reduce_scatter | solution.py:120
  323.2 4.1 collective-permute-start.4
  327.3 0.6 copy-start.2
  328.0 4.1 collective-permute-start.5
  328.0 4.1 collective-permute-start.12
  332.1 4.7 copy-start.4
  332.1 4.1 collective-permute-start.6
  332.1 0.7 copy-start.3
  332.8 4.0 collective-permute-start.13
  336.2 5.9 %copy-start.6 = (bf16[16,2,1664]{2,0,1:T(8,128)(2,1)}, bf16[16,2,1664]{2,0,1:T(8,128)(2,1)S(1)}, u32[]{:S(2)}) copy-start(bf16[16,2,1664]{2,0,1:T(8,128)(2,1)S(1)} %collective-permute-done.6) | copy-start | bytes 319492
  336.2 5.2 collective-permute-start.7
  336.8 3.1 copy-start.5
  336.8 5.4 collective-permute-start.14
  341.5 3.8 copy-start.7
  341.5 5.4 %collective-permute-start.8 = (bf16[16,2,1664]{2,0,1:T(8,128)(2,1)S(1)}, bf16[16,2,1664]{2,0,1:T(8,128)(2,1)}, u32[]{:S(2)}, u32[]{:S(2)}) collective-permute-start(bf16[16,2,1664]{2,0,1:T(8,128)(2,1)S(1)} %collective-permute-done.7), channel_id=1, source_target_pairs={{0,1},{1,2},{2,3},{3,4},{4,5},{5,6},{6,7},{7,8},{8,9},{9,10},{10,1... | collective-permute-start | bytes 319496 | tf_op jit(solution)/shard_map/ppermute | solution.py:23
  342.2 5.7 %collective-permute-start.15 = (bf16[16,2,1664]{2,0,1:T(8,128)(2,1)}, bf16[16,2,1664]{2,0,1:T(8,128)(2,1)}, u32[]{:S(2)}, u32[]{:S(2)}) collective-permute-start(bf16[16,2,1664]{2,0,1:T(8,128)(2,1)} %collective-permute-done.14), channel_id=1, source_target_pairs={{1,0},{2,1},{3,2},{4,3},{5,4},{6,5},{7,6},{8,7},{9,8},{10,9},{11,1... | collective-permute-start | bytes 319496 | tf_op jit(solution)/shard_map/ppermute | solution.py:25
  346.9 5.7 %collective-permute-start.9 = (bf16[16,2,1664]{2,0,1:T(8,128)(2,1)}, bf16[16,2,1664]{2,0,1:T(8,128)(2,1)}, u32[]{:S(2)}, u32[]{:S(2)}) collective-permute-start(bf16[16,2,1664]{2,0,1:T(8,128)(2,1)} %collective-permute-done.8), channel_id=1, source_target_pairs={{0,1},{1,2},{2,3},{3,4},{4,5},{5,6},{6,7},{7,8},{8,9},{9,10},{10,1... | collective-permute-start | bytes 319496 | tf_op jit(solution)/shard_map/ppermute | solution.py:23
  347.9 5.6 %collective-permute-start.16 = (bf16[16,2,1664]{2,0,1:T(8,128)(2,1)}, bf16[16,2,1664]{2,0,1:T(8,128)(2,1)S(1)}, u32[]{:S(2)}, u32[]{:S(2)}) collective-permute-start(bf16[16,2,1664]{2,0,1:T(8,128)(2,1)} %collective-permute-done.15), channel_id=1, source_target_pairs={{1,0},{2,1},{3,2},{4,3},{5,4},{6,5},{7,6},{8,7},{9,8},{10,9},{11,1... | collective-permute-start | bytes 319496 | tf_op jit(solution)/shard_map/ppermute | solution.py:25
  352.6 5.6 %collective-permute-start.10 = (bf16[16,2,1664]{2,0,1:T(8,128)(2,1)}, bf16[16,2,1664]{2,0,1:T(8,128)(2,1)S(1)}, u32[]{:S(2)}, u32[]{:S(2)}) collective-permute-start(bf16[16,2,1664]{2,0,1:T(8,128)(2,1)} %collective-permute-done.9), channel_id=1, source_target_pairs={{0,1},{1,2},{2,3},{3,4},{4,5},{5,6},{6,7},{7,8},{8,9},{9,10},{10,1... | collective-permute-start | bytes 319496 | tf_op jit(solution)/shard_map/ppermute | solution.py:23
  353.4 5.3 collective-permute-start.17
  358.1 5.3 collective-permute-start.11
  358.7 23.4 %collective-permute-start.18 = (bf16[16,2,1664]{2,0,1:T(8,128)(2,1)S(1)}, bf16[16,2,1664]{2,0,1:T(8,128)(2,1)S(1)}, u32[]{:S(2)}, u32[]{:S(2)}) collective-permute-start(bf16[16,2,1664]{2,0,1:T(8,128)(2,1)S(1)} %collective-permute-done.17), channel_id=1, source_target_pairs={{1,0},{2,1},{3,2},{4,3},{5,4},{6,5},{7,6},{8,7},{9,8},{10,9},{11,1... | collective-permute-start | bytes 319496 | tf_op jit(solution)/shard_map/ppermute | solution.py:25
  387.8 2.0 copy-start.10
  391.9 102.8 %copy-start.9 = (s32[1024]{0:T(1024)S(1)}, s32[1024]{0:T(1024)}, u32[]{:S(2)}) copy-start(s32[1024]{0:T(1024)} %param.8) | copy-start | bytes 12292
  391.9 106.3 %copy-start.8 = (s32[16,1024]{1,0:T(8,128)S(1)}, s32[16,1024]{1,0:T(8,128)}, u32[]{:S(2)}) copy-start(s32[16,1024]{1,0:T(8,128)} %param.7) | copy-start | bytes 196612
  478.8 1.3 collective-permute-start.19
  480.0 4.4 collective-permute-start.20
  484.4 5.3 collective-permute-start.21
  489.7 8.5 %collective-permute-start.22 = (f32[16,1024]{1,0:T(8,128)S(1)}, f32[16,1024]{1,0:T(8,128)S(1)}, u32[]{:S(2)}, u32[]{:S(2)}) collective-permute-start(f32[16,1024]{1,0:T(8,128)S(1)} %add_select_fusion.1), channel_id=1, source_target_pairs={{0,8},{1,9},{2,10},{3,11},{4,12},{5,13},{6,14},{7,15},{8,0},{9,1},... | collective-permute-start | bytes 196616 | tf_op jit(solution)/shard_map/ppermute | solution.py:35
Sparse Core Ops, SparseCore 0:
  93.5 60.0 reduce-scatter.3
  272.2 49.8 reduce-scatter.5
  392.0 83.1 reduce-scatter.7
